TPU v7x, 32 devices: a whole 2x2x4 slice. The times are simulated.
32 devices in a mesh: dp: 8 (over z, y), mp: 4 (over x, core).
Axes of the slice: x: 2, y: 2, z: 4, core: 2. Of those that a mesh axis runs over, the one named last changes fastest.
Arguments:
- tokens: bfloat16 [16560, 1024], P('dp'), may hold values from -6 to 6
- offsets: int32 [48, 5], P('dp'), may hold values from 0 to 308, as said below
- first_gain: float32 [1024], replicated, may hold values from 0.1 to 1.9
- first_shift: float32 [1024], replicated, may hold values from -1.8 to 1.8
- qkv_weight: float32 [1024, 3, 1024], P('dp', None, 'mp'), may hold values from -0.1875 to 0.1875
- qv_bias: float32 [2, 1024], P(None, 'mp'), may hold values from -1.8 to 1.8
- proj_weight: float32 [1024, 1024], P('mp', 'dp'), may hold values from -0.5 to 0.5
- proj_bias: float32 [1024], replicated, may hold values from -1.8 to 1.8
- second_gain: float32 [1024], replicated, may hold values from 0.1 to 1.9
- second_shift: float32 [1024], replicated, may hold values from -1.8 to 1.8
- expand_weight: float32 [1024, 4096], P('dp', 'mp'), may hold values from -0.1875 to 0.1875
- expand_bias: float32 [4096], P('mp'), may hold values from -1.8 to 1.8
- shrink_weight: float32 [4096, 1024], P('mp', 'dp'), may hold values from -0.09375 to 0.09375
- shrink_bias: float32 [1024], replicated, may hold values from -1.8 to 1.8
- cotangent: bfloat16 [16560, 1024], P('dp'), may hold values from -6 to 6
Outputs:
- out: bfloat16 [16560, 1024], P('dp')
- d_tokens: float32 [16560, 1024], P('dp')
- d_first_gain: float32 [1024], replicated
- d_first_shift: float32 [1024], replicated
- d_qkv_weight: float32 [1024, 3, 1024], P('dp', None, 'mp')
- d_qv_bias: float32 [2, 1024], P(None, 'mp')
- d_proj_weight: float32 [1024, 1024], P('mp', 'dp')
- d_proj_bias: float32 [1024], replicated
- d_second_gain: float32 [1024], replicated
- d_second_shift: float32 [1024], replicated
- d_expand_weight: float32 [1024, 4096], P('dp', 'mp')
- d_expand_bias: float32 [4096], P('mp')
- d_shrink_weight: float32 [4096, 1024], P('mp', 'dp')
- d_shrink_bias: float32 [1024], replicated
Inputs may be any that keep to these rules, and one draw needn't show every extreme that they name: `offsets`: each row lists, rising, where the 5 crops of one crop set start within its 345 tokens: the first starts at 0, one crop spans 197 tokens, the others 37 each, and the last ends at the set's end.
All inputs are finite; a program needn't handle non-finite values.
Results may differ from a plain program's by a relative error of at most 0.015.
Values may be sent and summed in bfloat16 or wider, within the bound.
No kernel may reach another device: no remote copies, remote signals or barrier semaphores. Data moves between devices by JAX's collectives and lax.ppermute only.
A program may use at most 128 MiB of HBM per device.

v0:
```python
import jax
import jax.numpy as jnp
from jax import lax
from jax.sharding import PartitionSpec as P

HEAD_DIM = 64
SET_TOKENS = 345
norm_eps = 1e-06
masked_score = -1e30
root_half = 0.7071067811865476


def layer_norm(values, gain, shift):
    centre = jnp.mean(values, axis=-1, keepdims=True)
    offset_rows = values - centre
    spread = jnp.mean(offset_rows * offset_rows, axis=-1, keepdims=True)
    return offset_rows * lax.rsqrt(spread + norm_eps) * gain + shift


def normalized(values):
    centre = jnp.mean(values, axis=-1, keepdims=True)
    offset_rows = values - centre
    spread = jnp.mean(offset_rows * offset_rows, axis=-1, keepdims=True)
    return offset_rows * lax.rsqrt(spread + norm_eps)


def gelu(values):
    return 0.5 * values * (1.0 + lax.erf(values * root_half))


def matmul(left, right):
    return jnp.dot(left, right, preferred_element_type=jnp.float32)


def set_scores(query_rows, key_rows, crop_ids, factor):
    scores = (
        jnp.einsum("qhe,khe->hqk", query_rows, key_rows, preferred_element_type=jnp.float32)
        * factor
    )
    same_crop = crop_ids[:, None] == crop_ids[None, :]
    return jnp.where(same_crop[None], scores, masked_score)


def attend_forward(factor):

    def attend(pieces):
        query_rows, key_rows, value_rows, crop_ids = pieces
        scores = set_scores(query_rows, key_rows, crop_ids, factor)
        peak_score = jnp.max(scores, axis=-1, keepdims=True)
        raised = jnp.exp(scores - peak_score)
        row_total = jnp.sum(raised, axis=-1, keepdims=True)
        weights = (raised / row_total).astype(jnp.bfloat16)
        mixed = jnp.einsum("hqk,khe->qhe", weights, value_rows, preferred_element_type=jnp.float32)
        return (mixed.astype(jnp.bfloat16), (peak_score + jnp.log(row_total))[..., 0])

    return attend


def attend_backward(factor):

    def backward(pieces):
        query_rows, key_rows, value_rows, crop_ids, log_total, grad_mixed = pieces
        scores = set_scores(query_rows, key_rows, crop_ids, factor)
        weights = jnp.exp(scores - log_total[..., None])
        grad_values = jnp.einsum(
            "hqk,qhe->khe",
            weights.astype(jnp.bfloat16),
            grad_mixed,
            preferred_element_type=jnp.float32,
        )
        grad_weights = jnp.einsum(
            "qhe,khe->hqk", grad_mixed, value_rows, preferred_element_type=jnp.float32
        )
        grad_scores = weights * (
            grad_weights - jnp.sum(weights * grad_weights, axis=-1, keepdims=True)
        )
        scores_low = grad_scores.astype(jnp.bfloat16)
        grad_queries = (
            jnp.einsum("hqk,khe->qhe", scores_low, key_rows, preferred_element_type=jnp.float32)
            * factor
        )
        grad_keys = (
            jnp.einsum("hqk,qhe->khe", scores_low, query_rows, preferred_element_type=jnp.float32)
            * factor
        )
        return (grad_queries, grad_keys, grad_values)

    return backward


def shards(
    tokens,
    offsets,
    first_gain,
    first_shift,
    qkv_weight,
    qv_bias,
    proj_weight,
    proj_bias,
    second_gain,
    second_shift,
    expand_weight,
    expand_bias,
    shrink_weight,
    shrink_bias,
    cotangent,
):
    row_count = tokens.shape[0]
    sets_here = offsets.shape[0]
    width_here = qkv_weight.shape[2]
    local_heads = width_here // HEAD_DIM
    factor = HEAD_DIM ** (-0.5)
    model_count = lax.axis_size("mp")
    model_index = lax.axis_index("mp")
    extra = -row_count % model_count
    share_rows = (row_count + extra) // model_count
    share_start = model_index * share_rows
    row_numbers = jnp.arange(row_count, dtype=jnp.int32)
    row_mask = ((row_numbers >= share_start) & (row_numbers < share_start + share_rows)).astype(
        jnp.float32
    )[:, None]
    positions = jnp.arange(SET_TOKENS, dtype=jnp.int32)
    crop_ids = jnp.sum((positions[None, :, None] >= offsets[:, None, :]).astype(jnp.int32), axis=-1)
    qkv_master = qkv_weight.astype(jnp.bfloat16)
    proj_master = proj_weight.astype(jnp.bfloat16)
    expand_master = expand_weight.astype(jnp.bfloat16)
    shrink_master = shrink_weight.astype(jnp.bfloat16)
    qkv_full, proj_full, expand_full, shrink_full = (
        lax.all_gather(qkv_master, "dp", axis=0, tiled=True),
        lax.all_gather(proj_master, "dp", axis=1, tiled=True),
        lax.all_gather(expand_master, "dp", axis=0, tiled=True),
        lax.all_gather(shrink_master, "dp", axis=1, tiled=True),
    )
    inputs = tokens.astype(jnp.float32)
    first_low = layer_norm(inputs, first_gain, first_shift).astype(jnp.bfloat16)
    projected = jnp.einsum("td,dcf->tcf", first_low, qkv_full, preferred_element_type=jnp.float32)
    shaped = (sets_here, SET_TOKENS, local_heads, HEAD_DIM)
    query_rows = (projected[:, 0] + qv_bias[0]).astype(jnp.bfloat16).reshape(shaped)
    key_rows = projected[:, 1].astype(jnp.bfloat16).reshape(shaped)
    value_rows = (projected[:, 2] + qv_bias[1]).astype(jnp.bfloat16).reshape(shaped)
    attended, log_total = lax.map(
        attend_forward(factor), (query_rows, key_rows, value_rows, crop_ids)
    )
    attended_flat = attended.reshape(row_count, width_here)
    attn_part = matmul(attended_flat, proj_full)
    residual = inputs + lax.psum(attn_part, "mp") + proj_bias
    second_low = layer_norm(residual, second_gain, second_shift).astype(jnp.bfloat16)
    hidden_pre = matmul(second_low, expand_full) + expand_bias
    hidden = gelu(hidden_pre).astype(jnp.bfloat16)
    mlp_part = matmul(hidden, shrink_full)
    outputs = (
        residual + lax.psum(mlp_part.astype(jnp.bfloat16), "mp").astype(jnp.float32) + shrink_bias
    ).astype(jnp.bfloat16)
    grad_out = cotangent.astype(jnp.float32)
    shrink_grad = jnp.einsum("tf,td->fd", hidden, cotangent, preferred_element_type=jnp.float32)
    grad_hidden = jnp.einsum(
        "td,fd->tf", cotangent, shrink_full, preferred_element_type=jnp.float32
    )
    _, gelu_pull = jax.vjp(gelu, hidden_pre)
    grad_pre = gelu_pull(grad_hidden)[0]
    expand_bias_grad = jnp.sum(grad_pre, axis=0)
    grad_pre_low = grad_pre.astype(jnp.bfloat16)
    expand_grad = jnp.einsum(
        "td,tf->df", second_low, grad_pre_low, preferred_element_type=jnp.float32
    )
    second_part = jnp.einsum(
        "tf,df->td", grad_pre_low, expand_full, preferred_element_type=jnp.float32
    )
    grad_second = lax.psum(second_part, "mp")
    _, second_pull = jax.vjp(lambda values: layer_norm(values, second_gain, second_shift), residual)
    grad_residual = second_pull(grad_second)[0] + grad_out
    grad_second_kept = grad_second * row_mask
    second_gain_grad = jnp.sum(grad_second_kept * normalized(residual), axis=0)
    second_shift_grad = jnp.sum(grad_second_kept, axis=0)
    proj_bias_grad = jnp.sum(grad_residual * row_mask, axis=0)
    shrink_bias_grad = jnp.sum(grad_out * row_mask, axis=0)
    residual_low = grad_residual.astype(jnp.bfloat16)
    proj_grad = jnp.einsum(
        "tc,td->cd", attended_flat, residual_low, preferred_element_type=jnp.float32
    )
    grad_attended = jnp.einsum(
        "td,cd->tc", residual_low, proj_full, preferred_element_type=jnp.float32
    ).astype(jnp.bfloat16)
    grad_queries, grad_keys, grad_values = lax.map(
        attend_backward(factor),
        (query_rows, key_rows, value_rows, crop_ids, log_total, grad_attended.reshape(shaped)),
    )
    grad_queries = grad_queries.reshape(row_count, width_here)
    grad_keys = grad_keys.reshape(row_count, width_here)
    grad_values = grad_values.reshape(row_count, width_here)
    qv_bias_grad = jnp.stack([jnp.sum(grad_queries, axis=0), jnp.sum(grad_values, axis=0)])
    grad_projected = jnp.stack([grad_queries, grad_keys, grad_values], axis=1).astype(jnp.bfloat16)
    qkv_grad = jnp.einsum(
        "td,tcf->dcf", first_low, grad_projected, preferred_element_type=jnp.float32
    )
    first_part = jnp.einsum(
        "tcf,dcf->td", grad_projected, qkv_full, preferred_element_type=jnp.float32
    )
    grad_first = lax.psum(first_part.astype(jnp.bfloat16), "mp").astype(jnp.float32)
    _, first_pull = jax.vjp(lambda values: layer_norm(values, first_gain, first_shift), inputs)
    grad_tokens = first_pull(grad_first)[0] + grad_residual
    grad_first_kept = grad_first * row_mask
    first_gain_grad = jnp.sum(grad_first_kept * normalized(inputs), axis=0)
    first_shift_grad = jnp.sum(grad_first_kept, axis=0)
    qkv_part, proj_part, expand_part, shrink_part = (
        lax.psum_scatter(
            qkv_grad.astype(jnp.bfloat16), "dp", scatter_dimension=0, tiled=True
        ).astype(jnp.float32),
        lax.psum_scatter(
            proj_grad.astype(jnp.bfloat16), "dp", scatter_dimension=1, tiled=True
        ).astype(jnp.float32),
        lax.psum_scatter(
            expand_grad.astype(jnp.bfloat16), "dp", scatter_dimension=0, tiled=True
        ).astype(jnp.float32),
        lax.psum_scatter(
            shrink_grad.astype(jnp.bfloat16), "dp", scatter_dimension=1, tiled=True
        ).astype(jnp.float32),
    )
    qv_part, expand_bias_part = lax.psum((qv_bias_grad, expand_bias_grad), "dp")
    small_parts = lax.psum(
        (
            first_gain_grad,
            first_shift_grad,
            proj_bias_grad,
            second_gain_grad,
            second_shift_grad,
            shrink_bias_grad,
        ),
        ("dp", "mp"),
    )
    return (
        outputs,
        grad_tokens,
        small_parts[0],
        small_parts[1],
        qkv_part,
        qv_part,
        proj_part,
        small_parts[2],
        small_parts[3],
        small_parts[4],
        expand_part,
        expand_bias_part,
        shrink_part,
        small_parts[5],
    )


def solution(mesh):
    placed = (
        P("dp", None),
        P("dp", None),
        P(),
        P(),
        P("dp", None, "mp"),
        P(None, "mp"),
        P("mp", "dp"),
        P(),
        P(),
        P(),
        P("dp", "mp"),
        P("mp"),
        P("mp", "dp"),
        P(),
        P("dp", None),
    )
    return jax.shard_map(
        shards,
        mesh=mesh,
        in_specs=placed,
        out_specs=(
            P("dp", None),
            P("dp", None),
            P(),
            P(),
            P("dp", None, "mp"),
            P(None, "mp"),
            P("mp", "dp"),
            P(),
            P(),
            P(),
            P("dp", "mp"),
            P("mp"),
            P("mp", "dp"),
            P(),
        ),
        check_vma=False,
    )
```

profile of v0, /device:TPU:0, one launch (start us, length us, event | category | flops | bytes accessed | tf_op | source)
XLA Modules:
  0.0 1080.6 jit_solution(10375636445222786847)
XLA Ops:
  11.9 3.0 convert_reduce_fusion
  16.9 34.5 %all_gather.13 = bf16[256,1024]{1,0:T(8,128)(2,1)} all-gather(bf16[256,128]{1,0:T(8,128)(2,1)S(1)} %convert_element_type.121), channel_id=1, replica_groups=mesh['dp'=8,'mp'=4] {'dp'}, dimensions={1}, use_global_device_ids=true | all-gather | bytes 589824 | tf_op jit(solution)/shard_map/all_gather | solution.py:130
  51.4 10.1 all-gather.4.cloned.1.call-done
  61.5 6.4 fusion.74
  72.6 3.0 squeeze.36
  76.2 4.4 reshape.221
  80.6 3.9 copy.95
  84.6 3.0 copy.89
  87.5 4.2 squeeze.35
  94.1 20.2 %while.26 = (s32[]{:T(128)}, bf16[6,345,4,64]{1,3,2,0:T(8,128)(2,1)}, f32[6,4,345]{2,1,0:T(4,128)}, bf16[6,345,4,64]{1,3,2,0:T(8,128)(2,1)S(1)}, s32[6,345]{1,0:...) while((s32[]{:T(128)}, ...), condition=%wide.region_6.7_spmd, body=%wide.region_3.6_spmd.sunk | while | flops 127800768 | bytes 7318627 | solution.py:141
  115.3 3.2 copy.96
  118.5 2.7 reshape.209
  121.2 6.1 fusion.87
  130.2 151.0 %all-reduce.7.cloned.1.call-done = f32[2070,1024]{1,0:T(8,128)} async-done(((f32[2070,1024]{1,0:T(8,128)}), f32[2070,1024]{1,0:T(8,128)}) %all-reduce.7.cloned.1.call-update) | async-done | bytes 8478736 | tf_op jit(solution)/shard_map/psum | solution.py:146
  281.3 5.8 fusion.82
  290.3 2.9 add_convert_fusion.1
  293.3 40.2 %all-gather.6.cloned.1.call-done = bf16[1024,1024]{1,0:T(8,128)(2,1)} async-done(((bf16[128,1024]{1,0:T(8,128)(2,1)}), bf16[1024,1024]{1,0:T(8,128)(2,1)}) %all-gather.6.cloned.1.call-update) | async-done | bytes 2097168 | tf_op jit(solution)/shard_map/all_gather | solution.py:131
  333.5 10.9 %fusion.88 = f32[2070,1024]{1,0:T(8,128)} fusion(bf16[2070,1024]{1,0:T(8,128)(2,1)} %add_convert_fusion.1, bf16[1024,1024]{1,0:T(8,128)(2,1)} %all-gather.6.cloned.1.call-done), kind=kOutput, calls=%fused_computation.143 | convolution fusion | flops 4341104640 | bytes 14815232 | tf_op jit(solution)/shard_map/dot_general | solution.py:32
  344.4 41.4 %all-gather.8.cloned.1.call-done = bf16[1024,1024]{1,0:T(8,128)(2,1)} async-done(((bf16[1024,128]{1,0:T(8,128)(2,1)}), bf16[1024,1024]{1,0:T(8,128)(2,1)}) %all-gather.8.cloned.1.call-update) | async-done | bytes 2097168 | tf_op jit(solution)/shard_map/all_gather | solution.py:132
  385.8 13.9 %fusion.80 = (f32[1024]{0:T(1024)}, bf16[2070,1024]{1,0:T(8,128)(2,1)S(1)}, bf16[2070,1024]{1,0:T(8,128)(2,1)}) fusion(f32[2070,1024]{1,0:T(8,128)} %fusion.88, f32[1024]{0:T(1024)S(1)} %copy-done.29, bf16[2070,1024]{1,0:T(8,128)(2,1)} %param.33, bf16[1024,1024]{1,0:T(8,128)(2,1)} %all-gather.8.cloned.1.call-done), kind=kOutput, calls=%fused_computation.136 | convolution fusion | flops 4377138176 | bytes 23302144 | tf_op jit(solution)/shard_map/td,fd->tf/dot_general | solution.py:156
  401.7 7.2 fusion.65
  408.9 9.5 convolution_convert_fusion.3
  418.4 3.9 copy.119
  422.5 9.2 fusion.67
  431.7 130.3 %all-reduce.9.cloned.1.call-done = f32[2070,1024]{1,0:T(8,128)} async-done(((f32[2070,1024]{1,0:T(8,128)}), f32[2070,1024]{1,0:T(8,128)}) %all-reduce.9.cloned.1.call-update) | async-done | bytes 8478736 | tf_op jit(solution)/shard_map/psum | solution.py:169
  562.0 8.2 multiply_reduce_fusion.1
  570.3 5.7 fusion.81
  576.0 3.4 copy-done.2
  583.3 4.0 copy.100
  587.3 46.0 %while.27 = (s32[]{:T(128)}, f32[6,345,4,64]{1,3,2,0:T(8,128)}, bf16[6,345,4,64]{1,3,2,0:T(8,128)(2,1)}, f32[6,345,4,64]{1,3,2,0:T(8,128)}, bf16[6,345,4,64]{1,3...) while((s32[]{:T(128)}, f32[6,345,4,64]{1,3,2,0:T(8,128)}, ...), condition=%wide.region_16.17_spmd, body=%wide.region_14.16_spmd.sunk | while | flops 309283200 | bytes 17905568 | solution.py:184
  633.3 7.1 fusion.70
  641.4 5.6 fusion.85
  647.0 4.0 copy.114
  656.6 3.9 copy.115
  660.6 2.5 reshape.215
  668.8 9.3 convolution_convert_fusion.4
  678.3 9.7 convolution_convert_fusion.1
  687.9 5.1 bitcast_convert_fusion
  695.0 8.4 reduce-scatter.11.cloned.1.call-done
  705.5 20.3 %all-reduce.1 = (f32[2,256]{1,0:T(2,128)}, f32[1024]{0:T(1024)}) all-reduce(f32[2,256]{1,0:T(2,128)S(1)} %pad_maximum_fusion, f32[1024]{0:T(1024)S(1)} %copy-done.25), channel_id=1, replica_groups=mesh['dp'=8,'mp'=4] {'dp'}, use_global_device_ids=true, to_apply=%region_27.28 | all-reduce | flops 1536 | bytes 12288 | tf_op jit(solution)/shard_map/psum | solution.py:219
  725.7 42.0 %reduce-scatter.13.cloned.1.call-done = bf16[128,256]{1,0:T(8,128)(2,1)} async-done(((bf16[1024,256]{1,0:T(8,128)(2,1)}), bf16[128,256]{1,0:T(8,128)(2,1)}) %reduce-scatter.13.cloned.1.call-update) | async-done | bytes 65552
  769.4 66.7 %reduce-scatter.9.cloned.1.call-done = bf16[128,3,256]{2,0,1:T(8,128)(2,1)} async-done(((bf16[1024,3,256]{2,0,1:T(8,128)(2,1)}), bf16[128,3,256]{2,0,1:T(8,128)(2,1)}) %reduce-scatter.9.cloned.1.call-update) | async-done | bytes 196624 | tf_op jit(solution)/shard_map/reduce_scatter | solution.py:206
  837.8 155.5 %all-reduce.11.cloned.1.call-done = (bf16[2070,1024]{1,0:T(8,128)(2,1)}, bf16[2070,1024]{1,0:T(8,128)(2,1)}) async-done(((bf16[2070,1024]{1,0:T(8,128)(2,1)}, bf16[2070,1024]{1,0:T(8,128)(2,1)}), (bf16[2070,1024]{1,0:T(8,128)(2,1)}, bf16[2070,1024]{1,0:T(8,128)(2,1)})) %all-reduce.11.cloned.1.call-update) | async-done | bytes 8478736 | tf_op jit(solution)/shard_map/psum | solution.py:152
  993.3 5.4 fusion.56
  998.8 13.9 %fusion.54 = (f32[1024]{0:T(1024)S(1)}, f32[1024]{0:T(1024)S(1)}, f32[1024]{0:T(1024)S(1)}, f32[2070]{0:T(1024)S(1)}, f32[1024]{0:T(1024)S(1)}) fusion(bf16[2070,1024]{1,0:T(8,128)(2,1)} %param.33, f32[2070]{0:T(1024)S(1)} %copy-done.15, f32[2070,1024]{1,0:T(8,128)} %copy-done.2, f32[2070]{0:T(1024)S(1)} %negate_multiply_fusion.1, ...), kind=kLoop, calls=%fused_computation.79 | loop fusion | flops 44507112 | bytes 21266960 | tf_op jit(solution)/shard_map/reduce_sum | solution.py:176
  1012.7 13.7 %add_add_fusion.2 = f32[2070,1024]{1,0:T(8,128)} fusion(bf16[2070,1024]{1,0:T(8,128)(2,1)} %param.19, bf16[2070,1024]{1,0:T(8,128)(2,1)} %get-tuple-element.235, f32[2070]{0:T(1024)S(1)} %negate_multiply_fusion, f32[2070]{0:T(1024)S(1)} %multiply_multiply_fusion, f32[1024]{0:T(1024)S(1)} %copy-done.21, f32[2070]{0:T(1024)S(1)} %copy-done.13, ...), kind=kLoop, calls=%fused_computation.86 | loop fusion | flops 27555840 | bytes 29721016 | tf_op jit(solution)/shard_map/add | solution.py:201
  1026.4 7.1 add_convert_fusion
  1033.5 40.0 %all-reduce = (f32[1024]{0:T(1024)}, f32[1024]{0:T(1024)}, f32[1024]{0:T(1024)}, f32[1024]{0:T(1024)}, f32[1024]{0:T(1024)}, /*index=5*/f32[1024]{0:T(1024)}) all-reduce(f32[1024]{0:T(1024)S(1)} %get-tuple-element.189, f32[1024]{0:T(1024)S(1)} %get-tuple-element.187, ...), channel_id=1, replica_groups=mesh['dp'=8,'mp'=4] {'dp','mp'}, use_global_device_ids=true, to_apply=%region_21.22 | all-reduce | flops 6144 | bytes 49152 | tf_op jit(solution)/shard_map/psum | solution.py:220
  (236 shorter events, 113.0 us)
Async XLA Ops:
  7.2 54.3 %all-gather.4.cloned.1.call-start = ((), (), s32[]{:S(2)}) async-start(), calls=%async_computation.4 | async-start | bytes 1769472 | tf_op jit(solution)/shard_map/all_gather | solution.py:129
  8.9 272.3 %all-reduce.7.cloned.1.call-start = ((), (), s32[]{:S(2)}) async-start(), calls=%async_computation.5 | async-start | bytes 16973824 | tf_op jit(solution)/shard_map/psum | solution.py:146
  10.7 4.2 copy-start.1
  11.9 49.6 %copy-start.20 = (f32[1024]{0:T(1024)S(1)}, f32[1024]{0:T(1024)}, u32[]{:S(2)}) copy-start(f32[1024]{0:T(1024)} %param.21) | copy-start | bytes 12292
  11.9 49.6 %copy-start.30 = (f32[1024]{0:T(1024)S(1)}, f32[1024]{0:T(1024)}, u32[]{:S(2)}) copy-start(f32[1024]{0:T(1024)} %param.22) | copy-start | bytes 12292
  15.0 53.0 %copy-start.10 = (f32[2070]{0:T(1024)}, f32[2070]{0:T(1024)S(1)}, u32[]{:S(2)}) copy-start(f32[2070]{0:T(1024)S(1)} %broadcast_multiply_fusion.1) | copy-start | bytes 24844
  16.3 0.6 copy-start.16
  16.9 51.1 %copy-start.12 = (f32[2070]{0:T(1024)}, f32[2070]{0:T(1024)S(1)}, u32[]{:S(2)}) copy-start(f32[2070]{0:T(1024)S(1)} %fusion.78) | copy-start | bytes 24844
  114.3 1.0 copy-start.5
  114.3 13.1 %copy-start.18 = (s32[6,345]{1,0:T(8,128)}, s32[6,345]{1,0:T(8,128)S(1)}, u32[]{:S(2)}) copy-start(s32[6,345]{1,0:T(8,128)S(1)} %get-tuple-element.473) | copy-start | bytes 24844
  121.2 6.2 copy-start.4
  127.4 1.0 copy-start.7
  127.4 1.9 copy-start.8
  127.4 153.9 %copy-start.26 = (f32[1024]{0:T(1024)S(1)}, f32[1024]{0:T(1024)}, u32[]{:S(2)}) copy-start(f32[1024]{0:T(1024)} %param.26) | copy-start | bytes 12292
  127.4 206.1 %all-gather.6.cloned.1.call-start = ((), (), s32[]{:S(2)}) async-start(), calls=%async_computation.6 | async-start | bytes 2359296 | tf_op jit(solution)/shard_map/all_gather | solution.py:131
  129.2 256.6 %all-gather.8.cloned.1.call-start = ((), (), s32[]{:S(2)}) async-start(), calls=%async_computation.7 | async-start | bytes 2359296 | tf_op jit(solution)/shard_map/all_gather | solution.py:132
  130.0 432.0 %all-reduce.9.cloned.1.call-start = ((), (), s32[]{:S(2)}) async-start(), calls=%async_computation.8 | async-start | bytes 16973824 | tf_op jit(solution)/shard_map/psum | solution.py:169
  287.1 3.3 copy-start
  287.1 3.2 copy-start.19
  287.1 3.2 copy-start.23
  293.3 92.5 %copy-start.29 = (f32[1024]{0:T(1024)S(1)}, f32[1024]{0:T(1024)}, u32[]{:S(2)}) copy-start(f32[1024]{0:T(1024)} %param.30) | copy-start | bytes 12292
  385.8 15.9 %copy-start.27 = (bf16[1024,1024]{1,0:T(8,128)(2,1)S(1)}, bf16[1024,1024]{1,0:T(8,128)(2,1)}, u32[]{:S(2)}) copy-start(bf16[1024,1024]{1,0:T(8,128)(2,1)} %all-gather.6.cloned.1.call-done) | copy-start | bytes 6291460
  399.7 2.0 copy-start.32
  408.8 284.2 %reduce-scatter.15.cloned.1.call-start = ((), (), s32[]{:S(2)}) async-start(), calls=%async_computation.12 | async-start | bytes 2359296
  422.4 281.1 %reduce-scatter.11.cloned.1.call-start = ((), (), s32[]{:S(2)}) async-start(), calls=%async_computation.10 | async-start | bytes 2359296 | tf_op jit(solution)/shard_map/reduce_scatter | solution.py:212
  422.5 139.5 %copy-start.14 = (f32[2070]{0:T(1024)}, f32[2070]{0:T(1024)S(1)}, u32[]{:S(2)}) copy-start(f32[2070]{0:T(1024)S(1)} %fusion.77) | copy-start | bytes 24844
  431.7 336.1 %reduce-scatter.13.cloned.1.call-start = ((), (), s32[]{:S(2)}) async-start(), calls=%async_computation.11 | async-start | bytes 589824
  562.0 8.3 copy-start.3
  562.0 17.4 %slice-start = ((s8[4243456]{0:T(1024)(128)(4,1)}), s8[4194304]{0:T(1024)(128)(4,1)S(1)}, s32[]{:S(2)}) async-start(s8[4243456]{0:T(1024)(128)(4,1)} %bitcast.139), calls=%async_computation.14 | async-start | bytes 8388608
  570.3 9.1 slice-start.1
  570.3 9.1 copy-start.6
  576.0 3.4 copy-start.2
  660.5 8.3 copy-start.11
  660.5 8.3 copy-start.13
  660.5 8.3 copy-start.21
  660.6 8.3 copy-start.31
  665.4 170.7 %reduce-scatter.9.cloned.1.call-start = ((), (), s32[]{:S(2)}) async-start(), calls=%async_computation.9 | async-start | bytes 1769472 | tf_op jit(solution)/shard_map/reduce_scatter | solution.py:206
  678.2 9.7 copy-start.9
  678.2 315.1 %all-reduce.11.cloned.1.call-start = ((), (), s32[]{:S(2)}) async-start(), calls=%async_computation.13 | async-start | bytes 16973824 | tf_op jit(solution)/shard_map/psum | solution.py:152
  678.2 9.7 copy-start.28
  693.0 12.4 %copy-start.25 = (f32[1024]{0:T(1024)S(1)}, f32[1024]{0:T(1024)}, u32[]{:S(2)}) copy-start(f32[1024]{0:T(1024)} %get-tuple-element.236) | copy-start | bytes 12292
  993.3 5.4 copy-start.17
  993.3 5.4 copy-start.15
  998.8 27.6 %slice-start.2 = ((s8[4243456]{0:T(1024)(128)(4,1)}), s8[49152]{0:T(1024)(128)(4,1)S(1)}, s32[]{:S(2)}) async-start(s8[4243456]{0:T(1024)(128)(4,1)} %bitcast.142), calls=%async_computation.16 | async-start | bytes 98304
  1012.7 13.7 %slice-start.3 = ((s8[4243456]{0:T(1024)(128)(4,1)}), s8[4194304]{0:T(1024)(128)(4,1)S(1)}, s32[]{:S(2)}) async-start(s8[4243456]{0:T(1024)(128)(4,1)} %bitcast.142), calls=%async_computation.17 | async-start | bytes 8388608
  1012.7 13.7 %copy-start.24 = (f32[1024]{0:T(1024)S(1)}, f32[1024]{0:T(1024)}, u32[]{:S(2)}) copy-start(f32[1024]{0:T(1024)} %param.32) | copy-start | bytes 12292
  1026.4 7.1 copy-start.22
Sparse Core Ops, SparseCore 0:
  10.8 50.6 all-gather.3
  127.6 153.6 all-reduce.6
  284.2 49.2 all-gather.5
  336.2 49.5 all-gather.7
  409.0 152.9 all-reduce.8
  565.4 67.6 reduce-scatter.14
  636.6 66.8 reduce-scatter.10
  706.8 60.8 reduce-scatter.12
  771.6 64.4 reduce-scatter.8
  839.1 154.1 all-reduce.10
where the time goes:
time: 1080 us
  waiting for transfers between devices  646 us (60%)
  matrix products  143 us (13%)
  other arithmetic  95.7 us (9%)
  blocking collectives  94.8 us (9%)
  local copies, waits for them, and re-layouts  85.2 us (8%)
  between operations  15 us (1%)
    psum x1, waiting for transfers between devices, shards(): lax.psum(mlp_part.astype(jnp.bfloat16), 'mp').astype(jnp.float32)  156 us
    psum x1, waiting for transfers between devices, shards(): residual = inputs + lax.psum(attn_part, 'mp') + proj_bias  151 us
    psum x1, waiting for transfers between devices, shards(): grad_second = lax.psum(second_part, 'mp')  130 us
    reduce_scatter x1, waiting for transfers between devices, shards(): lax.psum_scatter(qkv_grad.astype(jnp.bfloat16), 'dp', scatter_dimension=0...  66.7 us
    unnamed x12, waiting for transfers between devices  42.2 us
    all_gather x1, waiting for transfers between devices, shards(): lax.all_gather(shrink_master, 'dp', axis=1, tiled=True)  41.4 us
    all_gather x1, waiting for transfers between devices, shards(): lax.all_gather(expand_master, 'dp', axis=0, tiled=True)  40.2 us
    psum x1, blocking collectives, shards(): lax.psum((first_gain_grad, first_shift_grad, proj_bias_grad, second_gain_...  40 us
  transfers between devices with their start and end apart: 10, of which 9 were waited for; matrix products, arithmetic and copies ran while one was open for 17% of the time, Pallas kernels for 0%

commit v1 on v0

--- a/solution.py
+++ b/solution.py
@@ -8,6 +8,33 @@
 norm_eps = 1e-06
 masked_score = -1e30
 root_half = 0.7071067811865476
+
+
+def _supply_boxes(local, array_axis):
+    tile_out = list(local.shape[1:])
+    tile_out[array_axis] *= local.shape[0]
+    base_arr = jnp.moveaxis(local, 0, array_axis).reshape(tile_out)
+    return base_arr
+
+
+def treat_marks(local_array, along_axis):
+    ready, u1 = (lax.axis_size(along_axis), lax.axis_index(along_axis))
+    taken_in, later = (local_array[None], 1)
+    while later < ready:
+        current_arr = lax.ppermute(
+            taken_in, along_axis, list(map(lambda m: (m, m ^ later), range(ready)))
+        )
+        opened = u1 & later == 0
+        taken_in = jnp.concatenate(
+            [jnp.where(opened, taken_in, current_arr), jnp.where(opened, current_arr, taken_in)]
+        )
+        later *= 2
+    return taken_in
+
+
+def write_masks_in(z, xin, on_dim):
+    frame_out = _supply_boxes(treat_marks(z, xin), on_dim)
+    return frame_out
 
 
 def layer_norm(values, gain, shift):
@@ -128,7 +155,7 @@
     qkv_full, proj_full, expand_full, shrink_full = (
         lax.all_gather(qkv_master, "dp", axis=0, tiled=True),
         lax.all_gather(proj_master, "dp", axis=1, tiled=True),
-        lax.all_gather(expand_master, "dp", axis=0, tiled=True),
+        write_masks_in(expand_master, "dp", on_dim=0),
         lax.all_gather(shrink_master, "dp", axis=1, tiled=True),
     )
     inputs = tokens.astype(jnp.float32)

time: 1080 us -> 990 us (0.917)
  waiting for transfers between devices: 646 us -> 544 us
    psum x1, waiting for transfers between devices: 151 us -> 69.7 us  [shards(): residual = inputs + lax.psum(attn_part, 'mp') + proj_bias]
    ppermute x0 -> x3, waiting for transfers between devices: none -> 61.3 us  [treat_marks(): lax.ppermute(taken_in, along_axis, list(map(lambda m: (m, m ^ later), ran...]
    all_gather x1, waiting for transfers between devices: 41.4 us -> 0.01 us  [shards(): lax.all_gather(shrink_master, 'dp', axis=1, tiled=True)]
    all_gather x1 -> x0, waiting for transfers between devices: 40.2 us -> none  [shards(): lax.all_gather(expand_master, 'dp', axis=0, tiled=True)]
    unnamed x81 -> x93, local copies, waits for them, and re-layouts: 22.8 us -> 21.3 us
    unnamed x12 -> x11, waiting for transfers between devices: 42.2 us -> 42.1 us
  transfers between devices with their start and end apart: 10 -> 12, of which waited for: 9 -> 10; matrix products, arithmetic and copies ran while one was open for 17% -> 25% of each run, Pallas kernels for 0% -> 0%
where the time goes in v1:
time: 990 us; the launch traced here: 985 us
  waiting for transfers between devices  544 us (55%)
  matrix products  148 us (15%)
  other arithmetic  95.6 us (10%)
  blocking collectives  93.8 us (9%)
  local copies, waits for them, and re-layouts  83 us (8%)
  between operations  14.8 us (1%)
    psum x1, waiting for transfers between devices, shards(): lax.psum(mlp_part.astype(jnp.bfloat16), 'mp').astype(jnp.float32)  156 us
    psum x1, waiting for transfers between devices, shards(): grad_second = lax.psum(second_part, 'mp')  129 us
    psum x1, waiting for transfers between devices, shards(): residual = inputs + lax.psum(attn_part, 'mp') + proj_bias  69.7 us
    reduce_scatter x1, waiting for transfers between devices, shards(): lax.psum_scatter(qkv_grad.astype(jnp.bfloat16), 'dp', scatter_dimension=0...  66.7 us
    ppermute x3, waiting for transfers between devices, treat_marks(): lax.ppermute(taken_in, along_axis, list(map(lambda m: (m, m ^ later), ran...  61.3 us
    unnamed x11, waiting for transfers between devices  42.1 us
    psum x1, blocking collectives, shards(): lax.psum((first_gain_grad, first_shift_grad, proj_bias_grad, second_gain_...  39.9 us
    all_gather x1, blocking collectives, shards(): lax.all_gather(proj_master, 'dp', axis=1, tiled=True)  33.5 us
  transfers between devices with their start and end apart: 12, of which 10 were waited for; matrix products, arithmetic and copies ran while one was open for 25% of the time, Pallas kernels for 0%

profile of v1, /device:TPU:0, one launch (start us, length us, event | category | flops | bytes accessed | tf_op | source)
XLA Modules:
  0.0 985.1 jit_solution(1317291148537597632)
XLA Ops:
  10.9 3.0 convert_reduce_fusion
  16.6 33.5 %all_gather.10 = bf16[256,1024]{1,0:T(8,128)(2,1)} all-gather(bf16[256,128]{1,0:T(8,128)(2,1)S(1)} %convert_element_type.121), channel_id=1, replica_groups=mesh['dp'=8,'mp'=4] {'dp'}, dimensions={1}, use_global_device_ids=true | all-gather | bytes 589824 | tf_op jit(solution)/shard_map/all_gather | solution.py:157
  50.2 10.6 %all-gather.3.cloned.1.call-done = bf16[1024,3,256]{2,0,1:T(8,128)(2,1)} async-done(((bf16[128,3,256]{2,0,1:T(8,128)(2,1)}), bf16[1024,3,256]{2,0,1:T(8,128)(2,1)}) %all-gather.3.cloned.1.call-update) | async-done | bytes 1572880 | tf_op jit(solution)/shard_map/all_gather | solution.py:156
  60.8 6.5 fusion.74
  71.9 3.0 squeeze.35
  76.6 3.0 copy.91
  79.5 3.0 squeeze.36
  83.2 4.6 reshape.225
  87.7 3.9 copy.95
  91.7 21.8 %while.26 = (s32[]{:T(128)}, bf16[6,345,4,64]{1,3,2,0:T(8,128)(2,1)S(1)}, f32[6,4,345]{2,1,0:T(4,128)}, bf16[6,345,4,64]{1,3,2,0:T(8,128)(2,1)}, s32[6,345]{1,0:...) while((s32[]{:T(128)}, ...), condition=%wide.region_6.7_spmd, body=%wide.region_3.6_spmd.sunk | while | flops 127800768 | bytes 7319127 | solution.py:168
  115.4 2.7 reshape.212
  118.2 6.1 fusion.87
  126.0 6.8 collective-permute-done
  135.4 10.6 %collective-permute-done.1 = bf16[2,128,1024]{2,1,0:T(8,128)(2,1)} collective-permute-done((bf16[2,128,1024]{2,1,0:T(8,128)(2,1)S(1)}, bf16[2,128,1024]{2,1,0:T(8,128)(2,1)}, u32[]{:S(2)}, u32[]{:S(2)}) %collective-permute-start.1) | collective-permute-done | bytes 524320 | tf_op jit(solution)/shard_map/ppermute | solution.py:24
  148.3 2.7 collective-permute-start.2
  151.0 43.9 %collective-permute-done.2 = bf16[4,128,1024]{2,1,0:T(8,128)(2,1)} collective-permute-done((bf16[4,128,1024]{2,1,0:T(8,128)(2,1)}, bf16[4,128,1024]{2,1,0:T(8,128)(2,1)}, u32[]{:S(2)}, u32[]{:S(2)}) %collective-permute-start.2) | collective-permute-done | bytes 1048608 | tf_op jit(solution)/shard_map/ppermute | solution.py:24
  197.8 11.1 %fusion.88 = f32[2070,1024]{1,0:T(8,128)} fusion(bf16[2070,1024]{1,0:T(8,128)(2,1)} %param.33, bf16[1024,1024]{1,0:T(8,128)(2,1)} %all-gather.5.cloned.1.call-done), kind=kOutput, calls=%fused_computation.153 | convolution fusion | flops 4341104640 | bytes 14815232 | tf_op jit(solution)/shard_map/td,fd->tf/dot_general | solution.py:183
  208.9 69.7 %all-reduce.7.cloned.1.call-done = f32[2070,1024]{1,0:T(8,128)} async-done(((f32[2070,1024]{1,0:T(8,128)}), f32[2070,1024]{1,0:T(8,128)}) %all-reduce.7.cloned.1.call-update) | async-done | bytes 8478736 | tf_op jit(solution)/shard_map/psum | solution.py:173
  278.6 5.8 fusion.82
  285.5 2.6 copy-done
  288.1 14.3 %fusion.80 = (f32[1024]{0:T(1024)}, bf16[2070,1024]{1,0:T(8,128)(2,1)S(1)}, bf16[2070,1024]{1,0:T(8,128)(2,1)}) fusion(f32[2070,1024]{1,0:T(8,128)} %fusion.88, f32[1024]{0:T(1024)S(1)} %copy-done.34, bf16[1024,1024]{1,0:T(8,128)(2,1)S(1)} %bitcast.147, f32[2070,1024]{1,0:T(8,128)S(1)} %get-tuple-element.241, f32[1024]{0:T(1024)S(1)} %copy-done.35, ...), kind=kOutput, calls=%fused_computation.146 | convolution fusion | flops 4387736576 | bytes 27566256 | tf_op jit(solution)/shard_map/dot_general | solution.py:59
  304.4 7.1 fusion.65
  311.7 9.2 convolution_convert_fusion.3
  320.9 4.0 copy.119
  325.0 12.1 %fusion.67 = bf16[1024,1024]{1,0:T(8,128)(2,1)} fusion(bf16[2070,1024]{1,0:T(8,128)(2,1)} %copy-done.38, f32[2070,1024]{1,0:T(8,128)} %copy-done, f32[1024]{0:T(1024)S(1)} %copy-done.35, f32[1024]{0:T(1024)S(1)} %copy-done.26, f32[2070]{0:T(1024)S(1)} %fusion.79, f32[2070]{0:T(1024)S(1)} %broadcast_multiply_fusion), kind=kOutput, calls=%fused_computation.111 | convolution fusion | flops 4352751616 | bytes 14839984 | tf_op jit(solution)/shard_map/td,tf->df/dot_general | solution.py:190
  337.6 128.8 %all-reduce.9.cloned.1.call-done = f32[2070,1024]{1,0:T(8,128)} async-done(((f32[2070,1024]{1,0:T(8,128)}), f32[2070,1024]{1,0:T(8,128)}) %all-reduce.9.cloned.1.call-update) | async-done | bytes 8478736 | tf_op jit(solution)/shard_map/psum | solution.py:196
  466.5 8.2 multiply_reduce_fusion.1
  474.8 5.7 fusion.81
  480.5 3.4 copy-done.2
  487.8 4.0 copy.100
  491.8 45.9 %while.27 = (s32[]{:T(128)}, f32[6,345,4,64]{1,3,2,0:T(8,128)}, bf16[6,345,4,64]{1,3,2,0:T(8,128)(2,1)}, f32[6,345,4,64]{1,3,2,0:T(8,128)}, bf16[6,345,4,64]{1,3...) while((s32[]{:T(128)}, f32[6,345,4,64]{1,3,2,0:T(8,128)}, ...), condition=%wide.region_16.17_spmd, body=%wide.region_14.16_spmd.sunk | while | flops 309283200 | bytes 17905560 | solution.py:211
  537.7 7.1 fusion.70
  545.8 5.6 fusion.85
  551.5 4.0 copy.114
  558.0 3.9 copy.115
  573.2 9.3 convolution_convert_fusion.4
  582.7 9.6 convolution_convert_fusion.1
  592.3 5.1 bitcast_convert_fusion
  599.3 8.7 reduce-scatter.11.cloned.1.call-done
  610.1 20.3 %all-reduce.1 = (f32[2,256]{1,0:T(2,128)}, f32[1024]{0:T(1024)}) all-reduce(f32[2,256]{1,0:T(2,128)S(1)} %pad_maximum_fusion.3, f32[1024]{0:T(1024)S(1)} %copy-done.29), channel_id=1, replica_groups=mesh['dp'=8,'mp'=4] {'dp'}, use_global_device_ids=true, to_apply=%region_27.28 | all-reduce | flops 1536 | bytes 12288 | tf_op jit(solution)/shard_map/psum | solution.py:246
  630.4 42.0 %reduce-scatter.13.cloned.1.call-done = bf16[128,256]{1,0:T(8,128)(2,1)} async-done(((bf16[1024,256]{1,0:T(8,128)(2,1)}), bf16[128,256]{1,0:T(8,128)(2,1)}) %reduce-scatter.13.cloned.1.call-update) | async-done | bytes 65552
  674.0 66.7 %reduce-scatter.9.cloned.1.call-done = bf16[128,3,256]{2,0,1:T(8,128)(2,1)} async-done(((bf16[1024,3,256]{2,0,1:T(8,128)(2,1)}), bf16[128,3,256]{2,0,1:T(8,128)(2,1)}) %reduce-scatter.9.cloned.1.call-update) | async-done | bytes 196624 | tf_op jit(solution)/shard_map/reduce_scatter | solution.py:233
  742.4 155.7 %all-reduce.11.cloned.1.call-done = (bf16[2070,1024]{1,0:T(8,128)(2,1)}, bf16[2070,1024]{1,0:T(8,128)(2,1)}) async-done(((bf16[2070,1024]{1,0:T(8,128)(2,1)}, bf16[2070,1024]{1,0:T(8,128)(2,1)}), (bf16[2070,1024]{1,0:T(8,128)(2,1)}, bf16[2070,1024]{1,0:T(8,128)(2,1)})) %all-reduce.11.cloned.1.call-update) | async-done | bytes 8478736 | tf_op jit(solution)/shard_map/psum | solution.py:179
  898.1 5.4 fusion.56
  903.5 14.0 %fusion.54 = (f32[1024]{0:T(1024)S(1)}, f32[1024]{0:T(1024)S(1)}, f32[1024]{0:T(1024)S(1)}, f32[2070]{0:T(1024)S(1)}, f32[1024]{0:T(1024)S(1)}) fusion(bf16[2070,1024]{1,0:T(8,128)(2,1)} %param.33, f32[2070]{0:T(1024)S(1)} %copy-done.20, f32[2070,1024]{1,0:T(8,128)} %copy-done.2, f32[2070]{0:T(1024)S(1)} %negate_multiply_fusion.1, ...), kind=kLoop, calls=%fused_computation.79 | loop fusion | flops 44507112 | bytes 21266960 | tf_op jit(solution)/shard_map/reduce_sum | solution.py:203
  917.5 13.7 %add_add_fusion.2 = f32[2070,1024]{1,0:T(8,128)} fusion(bf16[2070,1024]{1,0:T(8,128)(2,1)} %param.19, bf16[2070,1024]{1,0:T(8,128)(2,1)} %get-tuple-element.235, f32[2070]{0:T(1024)S(1)} %negate_multiply_fusion, f32[2070]{0:T(1024)S(1)} %multiply_multiply_fusion, f32[1024]{0:T(1024)S(1)} %copy-done.25, f32[2070]{0:T(1024)S(1)} %copy-done.18, ...), kind=kLoop, calls=%fused_computation.86 | loop fusion | flops 27555840 | bytes 29721016 | tf_op jit(solution)/shard_map/add | solution.py:228
  931.2 7.1 add_convert_fusion
  938.3 39.9 %all-reduce = (f32[1024]{0:T(1024)}, f32[1024]{0:T(1024)}, f32[1024]{0:T(1024)}, f32[1024]{0:T(1024)}, f32[1024]{0:T(1024)}, /*index=5*/f32[1024]{0:T(1024)}) all-reduce(f32[1024]{0:T(1024)S(1)} %get-tuple-element.189, f32[1024]{0:T(1024)S(1)} %get-tuple-element.187, ...), channel_id=1, replica_groups=mesh['dp'=8,'mp'=4] {'dp','mp'}, use_global_device_ids=true, to_apply=%region_21.22 | all-reduce | flops 6144 | bytes 49152 | tf_op jit(solution)/shard_map/psum | solution.py:247
  (256 shorter events, 121.8 us)
Async XLA Ops:
  7.2 53.6 %all-gather.3.cloned.1.call-start = ((), (), s32[]{:S(2)}) async-start(), calls=%async_computation.4 | async-start | bytes 1769472 | tf_op jit(solution)/shard_map/all_gather | solution.py:156
  8.9 188.8 %all-gather.5.cloned.1.call-start = ((), (), s32[]{:S(2)}) async-start(), calls=%async_computation.6 | async-start | bytes 2359296 | tf_op jit(solution)/shard_map/all_gather | solution.py:159
  10.8 267.8 %all-reduce.7.cloned.1.call-start = ((), (), s32[]{:S(2)}) async-start(), calls=%async_computation.5 | async-start | bytes 16973824 | tf_op jit(solution)/shard_map/psum | solution.py:173
  10.9 5.4 copy-start.32
  10.9 5.6 copy-start.30
  10.9 5.7 copy-start.16
  10.9 49.9 %copy-start.24 = (f32[1024]{0:T(1024)S(1)}, f32[1024]{0:T(1024)}, u32[]{:S(2)}) copy-start(f32[1024]{0:T(1024)} %param.21) | copy-start | bytes 12292
  10.9 49.9 %copy-start.36 = (f32[1024]{0:T(1024)S(1)}, f32[1024]{0:T(1024)}, u32[]{:S(2)}) copy-start(f32[1024]{0:T(1024)} %param.22) | copy-start | bytes 12292
  14.3 46.4 %copy-start.14 = (f32[2070]{0:T(1024)}, f32[2070]{0:T(1024)S(1)}, u32[]{:S(2)}) copy-start(f32[2070]{0:T(1024)S(1)} %broadcast_multiply_fusion.1) | copy-start | bytes 24844
  16.2 44.5 %copy-start.17 = (f32[2070]{0:T(1024)}, f32[2070]{0:T(1024)S(1)}, u32[]{:S(2)}) copy-start(f32[2070]{0:T(1024)S(1)} %fusion.78) | copy-start | bytes 24844
  82.9 8.8 copy-start.12
  113.5 10.8 %copy-start.23 = (s32[6,345]{1,0:T(8,128)}, s32[6,345]{1,0:T(8,128)S(1)}, u32[]{:S(2)}) copy-start(s32[6,345]{1,0:T(8,128)S(1)} %get-tuple-element.479) | copy-start | bytes 24844
  118.1 6.2 copy-start.4
  124.3 342.1 %all-reduce.9.cloned.1.call-start = ((), (), s32[]{:S(2)}) async-start(), calls=%async_computation.7 | async-start | bytes 16973824 | tf_op jit(solution)/shard_map/psum | solution.py:196
  125.4 7.5 collective-permute-start
  133.7 12.3 %collective-permute-start.1 = (bf16[2,128,1024]{2,1,0:T(8,128)(2,1)S(1)}, bf16[2,128,1024]{2,1,0:T(8,128)(2,1)}, u32[]{:S(2)}, u32[]{:S(2)}) collective-permute-start(bf16[2,128,1024]{2,1,0:T(8,128)(2,1)S(1)} %pad_maximum_fusion.2), channel_id=1, source_target_pairs={{0,8},{4,12},{8,0},{12,4},{16,24},{20,28},{24,16},{28,20},{1,9},{5... | collective-permute-start | bytes 1572872 | tf_op jit(solution)/shard_map/ppermute | solution.py:24
  148.3 46.6 %collective-permute-start.2 = (bf16[4,128,1024]{2,1,0:T(8,128)(2,1)}, bf16[4,128,1024]{2,1,0:T(8,128)(2,1)}, u32[]{:S(2)}, u32[]{:S(2)}) collective-permute-start(bf16[4,128,1024]{2,1,0:T(8,128)(2,1)} %pad_maximum_fusion.1), channel_id=1, source_target_pairs={{0,16},{4,20},{8,24},{12,28},{16,0},{20,4},{24,8},{28,12},{1,17},{... | collective-permute-start | bytes 3145736 | tf_op jit(solution)/shard_map/ppermute | solution.py:24
  197.8 80.8 %copy-start.31 = (f32[1024]{0:T(1024)S(1)}, f32[1024]{0:T(1024)}, u32[]{:S(2)}) copy-start(f32[1024]{0:T(1024)} %param.26) | copy-start | bytes 12292
  284.4 3.6 copy-start
  284.4 3.6 copy-start.11
  284.4 3.6 copy-start.26
  284.4 3.6 copy-start.34
  284.5 3.6 copy-start.35
  311.5 285.9 %reduce-scatter.15.cloned.1.call-start = ((), (), s32[]{:S(2)}) async-start(), calls=%async_computation.11 | async-start | bytes 2359296
  324.9 283.2 %reduce-scatter.11.cloned.1.call-start = ((), (), s32[]{:S(2)}) async-start(), calls=%async_computation.9 | async-start | bytes 2359296 | tf_op jit(solution)/shard_map/reduce_scatter | solution.py:239
  325.0 141.5 %copy-start.19 = (f32[2070]{0:T(1024)}, f32[2070]{0:T(1024)S(1)}, u32[]{:S(2)}) copy-start(f32[2070]{0:T(1024)S(1)} %fusion.77) | copy-start | bytes 24844
  337.1 335.2 %reduce-scatter.13.cloned.1.call-start = ((), (), s32[]{:S(2)}) async-start(), calls=%async_computation.10 | async-start | bytes 589824
  466.4 8.3 copy-start.3
  466.4 17.4 %slice-start = ((s8[4243456]{0:T(1024)(128)(4,1)}), s8[4194304]{0:T(1024)(128)(4,1)S(1)}, s32[]{:S(2)}) async-start(s8[4243456]{0:T(1024)(128)(4,1)} %bitcast.142), calls=%async_computation.13 | async-start | bytes 8388608
  474.8 9.1 slice-start.1
  474.8 9.1 copy-start.10
  566.0 5.1 copy-start.5
  566.0 7.2 copy-start.15
  566.0 7.2 copy-start.18
  566.0 7.2 copy-start.25
  566.0 7.2 copy-start.37
  568.6 3.6 copy-start.6
  571.0 169.7 %reduce-scatter.9.cloned.1.call-start = ((), (), s32[]{:S(2)}) async-start(), calls=%async_computation.8 | async-start | bytes 1769472 | tf_op jit(solution)/shard_map/reduce_scatter | solution.py:233
  582.6 9.7 copy-start.13
  582.6 315.5 %all-reduce.11.cloned.1.call-start = ((), (), s32[]{:S(2)}) async-start(), calls=%async_computation.12 | async-start | bytes 16973824 | tf_op jit(solution)/shard_map/psum | solution.py:179
  582.6 9.6 copy-start.33
  597.3 12.7 %copy-start.29 = (f32[1024]{0:T(1024)S(1)}, f32[1024]{0:T(1024)}, u32[]{:S(2)}) copy-start(f32[1024]{0:T(1024)} %get-tuple-element.236) | copy-start | bytes 12292
  898.1 5.4 copy-start.22
  898.1 5.4 copy-start.20
  903.5 27.7 %slice-start.2 = ((s8[4243456]{0:T(1024)(128)(4,1)}), s8[49152]{0:T(1024)(128)(4,1)S(1)}, s32[]{:S(2)}) async-start(s8[4243456]{0:T(1024)(128)(4,1)} %bitcast.145), calls=%async_computation.15 | async-start | bytes 98304
  917.5 13.7 %slice-start.3 = ((s8[4243456]{0:T(1024)(128)(4,1)}), s8[4194304]{0:T(1024)(128)(4,1)S(1)}, s32[]{:S(2)}) async-start(s8[4243456]{0:T(1024)(128)(4,1)} %bitcast.145), calls=%async_computation.16 | async-start | bytes 8388608
  917.5 13.7 %copy-start.28 = (f32[1024]{0:T(1024)S(1)}, f32[1024]{0:T(1024)}, u32[]{:S(2)}) copy-start(f32[1024]{0:T(1024)} %param.32) | copy-start | bytes 12292
  931.2 7.1 copy-start.27
  (7 other events, 12.0 us)
Sparse Core Ops, SparseCore 0:
  10.8 49.9 all-gather.2
  63.4 50.3 all-gather.4
  124.5 154.0 all-reduce.6
  311.6 154.8 all-reduce.8
  469.8 67.8 reduce-scatter.14
  541.1 66.9 reduce-scatter.10
  611.4 60.8 reduce-scatter.12
  676.2 64.4 reduce-scatter.8
  743.9 154.1 all-reduce.10
